TPU v7x, 32 devices: a whole 2x2x4 slice. The times are simulated.
32 devices in a mesh: row: 8 (over z, y), col: 4 (over x, core).
Axes of the slice: x: 2, y: 2, z: 4, core: 2. Of those that a mesh axis runs over, the one named last changes fastest.
Arguments:
- query_acts: bfloat16 [256, 8192], P('col', 'row'), may hold values from -6 to 6
- query_grads: bfloat16 [256, 28672], P('row', 'col'), may hold values from -6 to 6
- ritz_mats: float32 [3, 8192, 28672], P(None, 'row', 'col'), may hold values from -0.095683193 to 0.095683193, as said below
- eigenvalues: float32 [3], replicated, may hold values from 0.5 to 4
- train_acts: bfloat16 [64, 8192], P('row'), may hold values from -6 to 6
- train_grads: bfloat16 [64, 28672], P('row', 'col'), may hold values from -6 to 6
Outputs:
- response: bfloat16 [64, 28672], P('row', 'col')
- scores: float32 [64], P('row')
Inputs may be any that keep to these rules, and one draw needn't show every extreme that they name: `ritz_mats`: real entries of order one over the square root of 8192; every matrix has full rank.
All inputs are finite; a program needn't handle non-finite values.
Results may differ from a plain program's by a relative error of at most 0.0012.
Values may be sent and summed in bfloat16 or wider, within the bound.
No kernel may reach another device: no remote copies, remote signals or barrier semaphores. Data moves between devices by JAX's collectives and lax.ppermute only.
A program may use at most 192 MiB of HBM per device.

v0:
```python
import math
import jax
import jax.numpy as jnp
from jax import lax
from jax.sharding import PartitionSpec as P

D_OUT = 28672
QUERY = 256
highest = lax.Precision.HIGHEST


def per_device(query_acts, query_grads, ritz_mats, eigenvalues, train_acts, train_grads):
    outer_cols = ritz_mats.shape[2]
    acts_all = lax.all_gather(query_acts, "col", axis=0, tiled=True)
    grad_tile = lax.dot_general(
        acts_all,
        lax.all_gather(query_grads, "row", axis=0, tiled=True),
        (((0,), (0,)), ((), ())),
        preferred_element_type=jnp.float32,
    )
    local_terms = jnp.sum(ritz_mats * grad_tile[None], axis=(1, 2))
    coeffs = lax.psum(local_terms, ("row", "col"))
    weights = coeffs / (eigenvalues * math.sqrt(QUERY * D_OUT))
    train_local = lax.all_to_all(train_acts, "row", split_axis=1, concat_axis=0, tiled=True).astype(
        jnp.float32
    )
    root_width = math.sqrt(D_OUT)
    total = jnp.zeros((lax.axis_size("row") * train_acts.shape[0], outer_cols), jnp.float32)
    for which in range(ritz_mats.shape[0]):
        total = total + weights[which] * jnp.dot(train_local, ritz_mats[which], precision=highest)
    response_full = lax.psum_scatter(total, "row", scatter_dimension=0, tiled=True)
    score_terms = jnp.sum(response_full * train_grads.astype(jnp.float32), axis=1) / root_width
    scores = lax.psum(score_terms, "col")
    response = response_full.astype(jnp.bfloat16)
    return (response, scores)


def solution(mesh):
    in_specs = (
        P("col", "row"),
        P("row", "col"),
        P(None, "row", "col"),
        P(),
        P("row", None),
        P("row", "col"),
    )
    out_specs = (P("row", "col"), P("row"))
    return jax.shard_map(
        per_device, mesh=mesh, in_specs=in_specs, out_specs=out_specs, check_vma=False
    )
```

profile of v0, /device:TPU:0, one launch (start us, length us, event | category | flops | bytes accessed | tf_op | source)
XLA Modules:
  0.0 306.3 jit_solution(11983988093099938950)
XLA Ops:
  7.2 0.0 all-gather.2.cloned.1.call-start
  7.2 0.7 all-gather.2.cloned.1.call-update
  7.9 8.9 %all_gather.6 = bf16[256,1024]{1,0:T(8,128)(2,1)S(1)} all-gather(bf16[64,1024]{1,0:T(8,128)(2,1)} %param.6), channel_id=1, replica_groups=mesh['row'=8,'col'=4] {'col'}, dimensions={0}, use_global_device_ids=true | all-gather | bytes 655360 | tf_op jit(solution)/shard_map/all_gather | solution.py:14
  16.8 62.4 %all-gather.2.cloned.1.call-done = bf16[256,7168]{1,0:T(8,128)(2,1)} async-done(((bf16[32,7168]{1,0:T(8,128)(2,1)}), bf16[256,7168]{1,0:T(8,128)(2,1)}) %all-gather.2.cloned.1.call-update) | async-done | bytes 3670032 | tf_op jit(solution)/shard_map/all_gather | solution.py:17
  79.1 13.7 %fusion.28 = f32[1024,7168]{1,0:T(8,128)} fusion(bf16[256,1024]{1,0:T(8,128)(2,1)S(1)} %all_gather.6, bf16[256,7168]{1,0:T(8,128)(2,1)} %all-gather.2.cloned.1.call-done), kind=kOutput, calls=%fused_computation.22 | convolution fusion | flops 3758096384 | bytes 33554432 | tf_op jit(solution)/shard_map/dot_general | solution.py:15
  92.8 0.0 copy-start.1
  92.8 35.5 %multiply_reduce_fusion = f32[3]{0:T(128)S(1)} fusion(f32[3,1024,7168]{2,1,0:T(8,128)} %param.8, f32[1024,7168]{1,0:T(8,128)} %fusion.28), kind=kLoop, calls=%fused_computation | loop fusion | flops 44040188 | bytes 117440528 | tf_op jit(solution)/shard_map/reduce_sum | solution.py:21
  128.4 3.4 %all-to-all-start = ((bf16[8,8,1024]{2,0,1:T(8,128)(2,1)}), bf16[8,8,1024]{2,0,1:T(8,128)(2,1)S(1)}, u32[]{:S(2)}, u32[]{:S(2)}) async-start(bf16[8,8,1024]{2,0,1:T(8,128)(2,1)} %bitcast.1), calls=%async_computation | async-start | bytes 262144 | tf_op jit(solution)/shard_map/all_to_all | solution.py:24
  131.8 0.0 reduce-scatter.2.cloned.1.call-start
  131.8 40.7 %psum.14 = f32[3]{0:T(128)S(1)} all-reduce(f32[3]{0:T(128)S(1)} %multiply_reduce_fusion), channel_id=1, replica_groups=mesh['row'=8,'col'=4] {'row','col'}, use_global_device_ids=true, to_apply=%region_1.0 | all-reduce | flops 3 | bytes 24 | tf_op jit(solution)/shard_map/psum | solution.py:22
  172.5 0.0 copy-done.1
  172.5 0.7 fusion.27
  173.2 0.0 all-to-all-done
  173.2 15.6 %fusion.15 = f32[64,7168]{1,0:T(8,128)S(1)} fusion(f32[3,1024,7168]{2,1,0:T(8,128)} %param.8, f32[]{:T(128)} %bitcast.5, bf16[8,8,1024]{2,0,1:T(8,128)(2,1)S(1)} %all-to-all-done), kind=kOutput, calls=%fused_computation.12 | convolution fusion | flops 5637603328 | bytes 31326720 | tf_op jit(solution)/shard_map/dot_general | solution.py:30
  188.8 18.0 %fusion.12 = f32[64,7168]{1,0:T(8,128)S(1)} fusion(f32[64,7168]{1,0:T(8,128)S(1)} %fusion.15, f32[3,1024,7168]{2,1,0:T(8,128)} %param.8, f32[]{:T(128)} %bitcast, bf16[8,8,1024]{2,0,1:T(8,128)(2,1)S(1)} %all-to-all-done), kind=kOutput, calls=%fused_computation.11 | convolution fusion | flops 5638062080 | bytes 33161728 | tf_op jit(solution)/shard_map/dot_general | solution.py:30
  206.8 0.0 copy-start
  206.8 17.5 %fusion.21 = f32[64,7168]{1,0:T(8,128)} fusion(f32[64,7168]{1,0:T(8,128)S(1)} %fusion.12, f32[3,1024,7168]{2,1,0:T(8,128)} %param.8, f32[]{:T(128)} %bitcast.8, bf16[8,8,1024]{2,0,1:T(8,128)(2,1)S(1)} %all-to-all-done), kind=kOutput, calls=%fused_computation.14 | convolution fusion | flops 5638062080 | bytes 33161728 | tf_op jit(solution)/shard_map/dot_general | solution.py:30
  224.3 0.0 reduce-scatter.2.cloned.1.call-update
  224.3 67.2 %reduce-scatter.2.cloned.1.call-done = f32[8,7168]{1,0:T(8,128)} async-done(((f32[64,7168]{1,0:T(8,128)}), f32[8,7168]{1,0:T(8,128)}) %reduce-scatter.2.cloned.1.call-update) | async-done | bytes 229392 | tf_op jit(solution)/shard_map/reduce_scatter | solution.py:31
  291.5 0.0 copy-done
  291.5 1.8 multiply_reduce_fusion.1
  293.3 6.2 %psum.15 = f32[8]{0:T(128)} all-reduce(f32[8]{0:T(128)S(1)} %broadcast_multiply_fusion), channel_id=1, replica_groups=mesh['row'=8,'col'=4] {'col'}, use_global_device_ids=true, to_apply=%region_4.0 | all-reduce | flops 8 | bytes 64 | tf_op jit(solution)/shard_map/psum | solution.py:33
  (2 shorter events, 0.0 us)
Async XLA Ops:
  7.2 72.0 %all-gather.2.cloned.1.call-start = ((), (), s32[]{:S(2)}) async-start(), calls=%async_computation.2 | async-start | bytes 4128768 | tf_op jit(solution)/shard_map/all_gather | solution.py:17
  92.8 79.7 %copy-start.1 = (f32[3]{0:T(128)S(1)}, f32[3]{0:T(128)}, u32[]{:S(2)}) copy-start(f32[3]{0:T(128)} %param.9) | copy-start | bytes 40
  128.4 44.8 %all-to-all-start = ((bf16[8,8,1024]{2,0,1:T(8,128)(2,1)}), bf16[8,8,1024]{2,0,1:T(8,128)(2,1)S(1)}, u32[]{:S(2)}, u32[]{:S(2)}) async-start(bf16[8,8,1024]{2,0,1:T(8,128)(2,1)} %bitcast.1), calls=%async_computation | async-start | bytes 262144 | tf_op jit(solution)/shard_map/all_to_all | solution.py:24
  131.8 159.8 %reduce-scatter.2.cloned.1.call-start = ((), (), s32[]{:S(2)}) async-start(), calls=%async_computation.3 | async-start | bytes 2064384 | tf_op jit(solution)/shard_map/reduce_scatter | solution.py:31
  206.8 84.7 %copy-start = (bf16[8,7168]{1,0:T(8,128)(2,1)S(1)}, bf16[8,7168]{1,0:T(8,128)(2,1)}, u32[]{:S(2)}) copy-start(bf16[8,7168]{1,0:T(8,128)(2,1)} %param.11) | copy-start | bytes 344068
Sparse Core Ops, SparseCore 0:
  10.2 68.9 all-gather.1
  224.4 67.0 reduce-scatter.1
where the time goes:
time: 307 us; the launch traced here: 306 us
  waiting for transfers between devices  130 us (42%)
  matrix products  64.8 us (21%)
  blocking collectives  55.7 us (18%)
  other arithmetic  37.4 us (12%)
  between operations  14.1 us (5%)
  starting transfers between devices  3.46 us (1%)
    reduce_scatter x1, waiting for transfers between devices, per_device(): lax.psum_scatter(total, 'row', scatter_dimension=0, tiled=True)  67.2 us
    all_gather x1, waiting for transfers between devices, per_device(): lax.all_gather(query_grads, 'row', axis=0, tiled=True)  62.4 us
    dot_general x3, matrix products, per_device(): jnp.dot(train_local, ritz_mats[which], precision=highest)  51.1 us
    psum x1, blocking collectives, per_device(): coeffs = lax.psum(local_terms, ('row', 'col'))  40.7 us
    reduce_sum x1, other arithmetic, per_device(): local_terms = jnp.sum(ritz_mats * grad_tile[None], axis=(1, 2))  35.5 us
    dot_general x1, matrix products, per_device(): lax.dot_general(acts_all, lax.all_gather(query_grads, 'row', axis=0, tile...  13.7 us
    all_gather x1, blocking collectives, per_device(): acts_all = lax.all_gather(query_acts, 'col', axis=0, tiled=True)  8.86 us
    psum x1, blocking collectives, per_device(): scores = lax.psum(score_terms, 'col')  6.17 us
  transfers between devices with their start and end apart: 3, of which 2 were waited for; matrix products, arithmetic and copies ran while one was open for 0% of the time, Pallas kernels for 0%

commit v1 on v0

--- a/solution.py
+++ b/solution.py
@@ -19,7 +19,7 @@
         preferred_element_type=jnp.float32,
     )
     local_terms = jnp.sum(ritz_mats * grad_tile[None], axis=(1, 2))
-    coeffs = lax.psum(local_terms, ("row", "col"))
+    coeffs = lax.psum(lax.psum(local_terms, "row"), "col")
     weights = coeffs / (eigenvalues * math.sqrt(QUERY * D_OUT))
     train_local = lax.all_to_all(train_acts, "row", split_axis=1, concat_axis=0, tiled=True).astype(
         jnp.float32

time: 307 us -> 293 us (0.954)
  blocking collectives: 55.7 us -> 40.3 us
    psum x1 -> x2, blocking collectives: 40.7 us -> 25.3 us  [per_device(): coeffs = lax.psum(lax.psum(local_terms, 'row'), 'col')]
  transfers between devices with their start and end apart: 3 -> 3, of which waited for: 2 -> 3; matrix products, arithmetic and copies ran while one was open for 0% -> 0% of each run, Pallas kernels for 0% -> 0%
where the time goes in v1:
time: 293 us; the launch traced here: 292 us
  waiting for transfers between devices  132 us (45%)
  matrix products  64.8 us (22%)
  blocking collectives  40.3 us (14%)
  other arithmetic  37.4 us (13%)
  between operations  14.1 us (5%)
  starting transfers between devices  3.45 us (1%)
    reduce_scatter x1, waiting for transfers between devices, per_device(): lax.psum_scatter(total, 'row', scatter_dimension=0, tiled=True)  68.1 us
    all_gather x1, waiting for transfers between devices, per_device(): lax.all_gather(query_grads, 'row', axis=0, tiled=True)  62.4 us
    dot_general x3, matrix products, per_device(): jnp.dot(train_local, ritz_mats[which], precision=highest)  51.1 us
    reduce_sum x1, other arithmetic, per_device(): local_terms = jnp.sum(ritz_mats * grad_tile[None], axis=(1, 2))  35.5 us
    psum x2, blocking collectives, per_device(): coeffs = lax.psum(lax.psum(local_terms, 'row'), 'col')  25.3 us
    dot_general x1, matrix products, per_device(): lax.dot_general(acts_all, lax.all_gather(query_grads, 'row', axis=0, tile...  13.7 us
    all_gather x1, blocking collectives, per_device(): acts_all = lax.all_gather(query_acts, 'col', axis=0, tiled=True)  8.86 us
    psum x1, blocking collectives, per_device(): scores = lax.psum(score_terms, 'col')  6.17 us
  transfers between devices with their start and end apart: 3, of which 3 were waited for; matrix products, arithmetic and copies ran while one was open for 0% of the time, Pallas kernels for 0%

profile of v1, /device:TPU:0, one launch (start us, length us, event | category | flops | bytes accessed | tf_op | source)
XLA Modules:
  0.0 292.3 jit_solution(13096004694386192556)
XLA Ops:
  7.2 0.0 all-gather.2.cloned.1.call-start
  7.2 0.7 all-gather.2.cloned.1.call-update
  7.9 8.9 %all_gather.6 = bf16[256,1024]{1,0:T(8,128)(2,1)S(1)} all-gather(bf16[64,1024]{1,0:T(8,128)(2,1)} %param.6), channel_id=1, replica_groups=mesh['row'=8,'col'=4] {'col'}, dimensions={0}, use_global_device_ids=true | all-gather | bytes 655360 | tf_op jit(solution)/shard_map/all_gather | solution.py:14
  16.8 62.4 %all-gather.2.cloned.1.call-done = bf16[256,7168]{1,0:T(8,128)(2,1)} async-done(((bf16[32,7168]{1,0:T(8,128)(2,1)}), bf16[256,7168]{1,0:T(8,128)(2,1)}) %all-gather.2.cloned.1.call-update) | async-done | bytes 3670032 | tf_op jit(solution)/shard_map/all_gather | solution.py:17
  79.1 13.7 %fusion.28 = f32[1024,7168]{1,0:T(8,128)} fusion(bf16[256,1024]{1,0:T(8,128)(2,1)S(1)} %all_gather.6, bf16[256,7168]{1,0:T(8,128)(2,1)} %all-gather.2.cloned.1.call-done), kind=kOutput, calls=%fused_computation.22 | convolution fusion | flops 3758096384 | bytes 33554432 | tf_op jit(solution)/shard_map/dot_general | solution.py:15
  92.8 0.0 copy-start.1
  92.8 35.5 %multiply_reduce_fusion = f32[3]{0:T(128)S(1)} fusion(f32[3,1024,7168]{2,1,0:T(8,128)} %param.8, f32[1024,7168]{1,0:T(8,128)} %fusion.28), kind=kLoop, calls=%fused_computation | loop fusion | flops 44040188 | bytes 117440528 | tf_op jit(solution)/shard_map/reduce_sum | solution.py:21
  128.4 19.2 %psum.21 = f32[3]{0:T(128)S(1)} all-reduce(f32[3]{0:T(128)S(1)} %multiply_reduce_fusion), channel_id=1, replica_groups=mesh['row'=8,'col'=4] {'row'}, use_global_device_ids=true, to_apply=%region_1.0 | all-reduce | flops 3 | bytes 24 | tf_op jit(solution)/shard_map/psum | solution.py:22
  147.5 3.4 %all-to-all-start = ((bf16[8,8,1024]{2,0,1:T(8,128)(2,1)}), bf16[8,8,1024]{2,0,1:T(8,128)(2,1)S(1)}, u32[]{:S(2)}, u32[]{:S(2)}) async-start(bf16[8,8,1024]{2,0,1:T(8,128)(2,1)} %bitcast.1), calls=%async_computation | async-start | bytes 262144 | tf_op jit(solution)/shard_map/all_to_all | solution.py:24
  150.9 0.0 reduce-scatter.2.cloned.1.call-start
  151.0 6.1 %psum.22 = f32[3]{0:T(128)S(1)} all-reduce(f32[3]{0:T(128)S(1)} %psum.21), channel_id=1, replica_groups=mesh['row'=8,'col'=4] {'col'}, use_global_device_ids=true, to_apply=%region_2.0 | all-reduce | flops 3 | bytes 24 | tf_op jit(solution)/shard_map/psum | solution.py:22
  157.1 0.0 copy-done.1
  157.1 0.7 fusion.27
  157.8 0.4 all-to-all-done
  158.2 15.6 %fusion.15 = f32[64,7168]{1,0:T(8,128)S(1)} fusion(f32[3,1024,7168]{2,1,0:T(8,128)} %param.8, f32[]{:T(128)} %bitcast.5, bf16[8,8,1024]{2,0,1:T(8,128)(2,1)S(1)} %all-to-all-done), kind=kOutput, calls=%fused_computation.12 | convolution fusion | flops 5637603328 | bytes 31326720 | tf_op jit(solution)/shard_map/dot_general | solution.py:30
  173.8 18.0 %fusion.12 = f32[64,7168]{1,0:T(8,128)S(1)} fusion(f32[64,7168]{1,0:T(8,128)S(1)} %fusion.15, f32[3,1024,7168]{2,1,0:T(8,128)} %param.8, f32[]{:T(128)} %bitcast, bf16[8,8,1024]{2,0,1:T(8,128)(2,1)S(1)} %all-to-all-done), kind=kOutput, calls=%fused_computation.11 | convolution fusion | flops 5638062080 | bytes 33161728 | tf_op jit(solution)/shard_map/dot_general | solution.py:30
  191.8 0.0 copy-start
  191.8 17.5 %fusion.21 = f32[64,7168]{1,0:T(8,128)} fusion(f32[64,7168]{1,0:T(8,128)S(1)} %fusion.12, f32[3,1024,7168]{2,1,0:T(8,128)} %param.8, f32[]{:T(128)} %bitcast.8, bf16[8,8,1024]{2,0,1:T(8,128)(2,1)S(1)} %all-to-all-done), kind=kOutput, calls=%fused_computation.14 | convolution fusion | flops 5638062080 | bytes 33161728 | tf_op jit(solution)/shard_map/dot_general | solution.py:30
  209.3 0.0 reduce-scatter.2.cloned.1.call-update
  209.3 68.1 %reduce-scatter.2.cloned.1.call-done = f32[8,7168]{1,0:T(8,128)} async-done(((f32[64,7168]{1,0:T(8,128)}), f32[8,7168]{1,0:T(8,128)}) %reduce-scatter.2.cloned.1.call-update) | async-done | bytes 229392 | tf_op jit(solution)/shard_map/reduce_scatter | solution.py:31
  277.5 0.0 copy-done
  277.5 1.8 multiply_reduce_fusion.1
  279.3 6.2 %psum.23 = f32[8]{0:T(128)} all-reduce(f32[8]{0:T(128)S(1)} %broadcast_multiply_fusion), channel_id=1, replica_groups=mesh['row'=8,'col'=4] {'col'}, use_global_device_ids=true, to_apply=%region_5.0 | all-reduce | flops 8 | bytes 64 | tf_op jit(solution)/shard_map/psum | solution.py:33
  (2 shorter events, 0.0 us)
Async XLA Ops:
  7.2 72.0 %all-gather.2.cloned.1.call-start = ((), (), s32[]{:S(2)}) async-start(), calls=%async_computation.2 | async-start | bytes 4128768 | tf_op jit(solution)/shard_map/all_gather | solution.py:17
  92.8 64.3 %copy-start.1 = (f32[3]{0:T(128)S(1)}, f32[3]{0:T(128)}, u32[]{:S(2)}) copy-start(f32[3]{0:T(128)} %param.9) | copy-start | bytes 40
  147.5 10.7 %all-to-all-start = ((bf16[8,8,1024]{2,0,1:T(8,128)(2,1)}), bf16[8,8,1024]{2,0,1:T(8,128)(2,1)S(1)}, u32[]{:S(2)}, u32[]{:S(2)}) async-start(bf16[8,8,1024]{2,0,1:T(8,128)(2,1)} %bitcast.1), calls=%async_computation | async-start | bytes 262144 | tf_op jit(solution)/shard_map/all_to_all | solution.py:24
  150.9 126.5 %reduce-scatter.2.cloned.1.call-start = ((), (), s32[]{:S(2)}) async-start(), calls=%async_computation.3 | async-start | bytes 2064384 | tf_op jit(solution)/shard_map/reduce_scatter | solution.py:31
  191.8 85.7 %copy-start = (bf16[8,7168]{1,0:T(8,128)(2,1)S(1)}, bf16[8,7168]{1,0:T(8,128)(2,1)}, u32[]{:S(2)}) copy-start(bf16[8,7168]{1,0:T(8,128)(2,1)} %param.11) | copy-start | bytes 344068
Sparse Core Ops, SparseCore 0:
  10.2 68.9 all-gather.1
  209.4 67.9 reduce-scatter.1
